TPU v7x, 128 devices: a whole 4x4x4 slice. The times are simulated.
128 devices in a mesh: req: 32 (over x, y, core), mlp: 4 (over z).
Axes of the slice: x: 4, y: 4, z: 4, core: 2. Of those that a mesh axis runs over, the one named last changes fastest.
Arguments:
- hidden_in: bfloat16 [64, 512, 2048], P('req'), may hold values from -6 to 6
- lengths: int32 [64], replicated, may hold values from 1 to 512, 16384 in all
- slot_request: int32 [64], replicated, may hold values from 0 to 63, each once
- adapter_of: int32 [64], replicated, may hold values from 0 to 63, as said below
- adapter_slot: int32 [64], replicated, may hold values from 0 to 63, each once
- norm_gain_attn: float32 [2048], replicated, may hold values from 0.5 to 1.5
- norm_gain_mlp: float32 [2048], replicated, may hold values from 0.5 to 1.5
- final_gain: float32 [2048], replicated, may hold values from 0.5 to 1.5
- w_qkv: bfloat16 [2048, 3, 2048], P(None, None, 'mlp')
- w_out: bfloat16 [2048, 2048], P('mlp'), may hold values from -0.125 to 0.125
- w_gateup: bfloat16 [2048, 2, 4096], P('req', None, 'mlp'), may hold values from -0.125 to 0.125
- w_down: bfloat16 [4096, 2048], P('mlp', 'req'), may hold values from -0.09375 to 0.09375
- adapter_down: bfloat16 [64, 16, 2048], P('req'), may hold values from -0.125 to 0.125
- adapter_up: bfloat16 [64, 16, 2048], P('req', None, 'mlp'), may hold values from -1.5 to 1.5
- vocab: bfloat16 [49152, 2048], P(('req', 'mlp')), may hold values from -0.375 to 0.375
Outputs:
- out_hidden: bfloat16 [64, 512, 2048], P('req')
- request_norm: float32 [64], replicated
- request_peak: float32 [64], replicated
Inputs may be any that keep to these rules, and one draw needn't show every extreme that they name: Some request has exactly 512 tokens, and all lengths together sum to 16384. `slot_request`: each request sits in exactly one slot. `adapter_of`: exactly 16 distinct adapters are named. `adapter_slot`: each adapter sits in exactly one row of the adapter tables.
All inputs are finite; a program needn't handle non-finite values.
Results may differ from a plain program's by a relative error of at most 0.018.
Values may be sent and summed in bfloat16 or wider, within the bound.
A program may use at most 128 MiB of HBM per device.

v0:
```python
import jax
import jax.numpy as jnp
from jax import lax
from jax.sharding import PartitionSpec as P

HEAD_WIDTH = 64


EPSILON = 1e-05
ROPE_BASE = 130000.0
ADAPTER_SCALE = 2.0
MASKED = -1e30


def rms_norm(values, gain):
    return values * lax.rsqrt(jnp.mean(values * values, axis=-1, keepdims=True) + EPSILON) * gain


def rotary_embedded(tensor):
    length = tensor.shape[-3]
    half_width = tensor.shape[-1] // 2
    frequency = ROPE_BASE ** (-(jnp.arange(half_width, dtype=jnp.float32) * 2.0 / tensor.shape[-1]))
    angles = jnp.arange(length, dtype=jnp.float32)[:, None] * frequency[None, :]
    cosine = jnp.cos(angles)[:, None, :]
    sine_part = jnp.sin(angles)[:, None, :]
    front_half = tensor[..., :half_width]
    back_half = tensor[..., half_width:]
    return jnp.concatenate(
        [front_half * cosine - back_half * sine_part, back_half * cosine + front_half * sine_part],
        axis=-1,
    )


def per_device(
    hidden_in,
    lengths,
    slot_request,
    adapter_of,
    adapter_slot,
    norm_gain_attn,
    norm_gain_mlp,
    final_gain,
    w_qkv,
    w_out,
    w_gateup,
    w_down,
    adapter_down,
    adapter_up,
    vocab,
):
    req_index = lax.axis_index("req")
    slots_number, sequence_length, width = hidden_in.shape
    row_count = slots_number * sequence_length
    head_cols = w_qkv.shape[2]
    heads_number = head_cols // HEAD_WIDTH
    unit_cols = w_gateup.shape[2]
    requests = lax.dynamic_slice_in_dim(slot_request, req_index * slots_number, slots_number)
    own_lengths = jnp.take(lengths, requests)
    own_adapters = jnp.take(adapter_of, requests)
    table_rows = jnp.take(adapter_slot, own_adapters)
    positions = jnp.arange(sequence_length, dtype=jnp.int32)
    residual_in = hidden_in.astype(jnp.float32)
    normed = rms_norm(residual_in, norm_gain_attn).astype(jnp.bfloat16)
    projected_rows = jnp.dot(
        normed.reshape(row_count, width),
        w_qkv.reshape(width, 3 * head_cols),
        preferred_element_type=jnp.float32,
    ).reshape(slots_number, sequence_length, 3, head_cols)
    down_all, up_all = (
        lax.all_gather(adapter_down, "req", axis=0, tiled=True),
        lax.all_gather(adapter_up, "req", axis=0, tiled=True),
    )
    down_rows = jnp.take(down_all, table_rows, axis=0)
    up_rows = jnp.take(up_all, table_rows, axis=0)
    low_rank = jnp.einsum(
        "bsd,brd->bsr", normed, down_rows, preferred_element_type=jnp.float32
    ).astype(jnp.bfloat16)
    raised_rows = jnp.einsum("bsr,brc->bsc", low_rank, up_rows, preferred_element_type=jnp.float32)
    queries = rotary_embedded(
        (projected_rows[:, :, 0] + ADAPTER_SCALE * raised_rows).reshape(
            slots_number, sequence_length, heads_number, HEAD_WIDTH
        )
    ).astype(jnp.bfloat16)
    key_heads = rotary_embedded(
        projected_rows[:, :, 1].reshape(slots_number, sequence_length, heads_number, HEAD_WIDTH)
    ).astype(jnp.bfloat16)
    value_heads = (
        projected_rows[:, :, 2]
        .reshape(slots_number, sequence_length, heads_number, HEAD_WIDTH)
        .astype(jnp.bfloat16)
    )
    causal = positions[None, :] <= positions[:, None]

    def attend(slot_items):
        query_one, key_one, value_one, length = slot_items
        scores = jnp.einsum(
            "qhd,khd->hqk", query_one, key_one, preferred_element_type=jnp.float32
        ) * HEAD_WIDTH ** (-0.5)
        allowed = causal & (positions[None, :] < length)
        scores = jnp.where(allowed[None], scores, MASKED)
        probabilities = jax.nn.softmax(scores, axis=-1).astype(jnp.bfloat16)
        return jnp.einsum(
            "hqk,khd->qhd", probabilities, value_one, preferred_element_type=jnp.float32
        ).astype(jnp.bfloat16)

    attended = lax.map(attend, (queries, key_heads, value_heads, own_lengths))
    head_part = jnp.dot(
        attended.reshape(row_count, head_cols), w_out, preferred_element_type=jnp.float32
    )
    mixed_heads = lax.psum(head_part.astype(jnp.bfloat16), "mlp").astype(jnp.float32)
    stream = (residual_in + mixed_heads.reshape(slots_number, sequence_length, width)).astype(
        jnp.bfloat16
    )
    normed_mid = (
        rms_norm(stream.astype(jnp.float32), norm_gain_mlp)
        .astype(jnp.bfloat16)
        .reshape(row_count, width)
    )
    shard_piece = lax.all_gather(w_gateup, "req", axis=0, tiled=True)
    gate_up = jnp.dot(
        normed_mid,
        shard_piece.reshape(shard_piece.shape[0], 2 * unit_cols),
        preferred_element_type=jnp.float32,
    )
    activated = (jax.nn.silu(gate_up[:, :unit_cols]) * gate_up[:, unit_cols:]).astype(jnp.bfloat16)
    unit_part = jnp.dot(
        activated,
        lax.all_gather(w_down, "req", axis=1, tiled=True),
        preferred_element_type=jnp.float32,
    )
    unit_total = lax.psum(unit_part.astype(jnp.bfloat16), "mlp").astype(jnp.float32)
    result = stream.astype(jnp.float32) + unit_total.reshape(slots_number, sequence_length, width)
    live = positions[None, :] < own_lengths[:, None]
    out_hidden = jnp.where(live[:, :, None], result, 0.0).astype(jnp.bfloat16)
    out_float = out_hidden.astype(jnp.float32)
    square_sum = jnp.sum(out_float * out_float, axis=(1, 2))
    slot_norm = jnp.sqrt(square_sum / (own_lengths.astype(jnp.float32) * width))
    picked = (positions[None, :] == own_lengths[:, None] - 1).astype(jnp.float32)
    last_rows = jnp.einsum("bs,bsd->bd", picked, out_float, precision=lax.Precision.HIGHEST)
    last_rounded = lax.optimization_barrier(rms_norm(last_rows, final_gain).astype(jnp.bfloat16))
    last_normed = last_rounded.astype(jnp.float32)
    every_last, every_norm = (
        lax.all_gather(last_normed, "req", axis=0, tiled=True),
        lax.all_gather(slot_norm, "req", axis=0, tiled=True),
    )
    logits = lax.dot_general(
        every_last.astype(jnp.bfloat16),
        vocab,
        (((1,), (1,)), ((), ())),
        preferred_element_type=jnp.float32,
    )
    slot_peak = lax.pmax(jnp.max(logits, axis=1), ("req", "mlp"))
    request_total = slot_request.shape[0]
    owners = slot_request[None, :] == jnp.arange(request_total, dtype=jnp.int32)[:, None]
    request_norm = jnp.sum(jnp.where(owners, every_norm[None, :], 0.0), axis=1)
    request_peak = jnp.sum(jnp.where(owners, slot_peak[None, :], 0.0), axis=1)
    return (out_hidden, request_norm, request_peak)


def solution(mesh):
    return jax.shard_map(
        per_device,
        mesh=mesh,
        in_specs=(
            P("req", None, None),
            P(),
            P(),
            P(),
            P(),
            P(),
            P(),
            P(),
            P(None, None, "mlp"),
            P("mlp", None),
            P("req", None, "mlp"),
            P("mlp", "req"),
            P("req", None, None),
            P("req", None, "mlp"),
            P(("req", "mlp"), None),
        ),
        out_specs=(P("req", None, None), P(), P()),
        check_vma=False,
    )
```

profile of v0, /device:TPU:0, one launch (start us, length us, event | category | flops | bytes accessed | tf_op | source)
XLA Modules:
  0.0 623.8 jit_solution(15625885839021791205)
XLA Ops:
  7.2 0.7 all-gather.8.cloned.1.call-update
  8.0 0.7 all-gather.6.cloned.1.call-update
  8.7 8.8 %copy.26 = bf16[2048,3,512]{0,2,1:T(8,128)(2,1)} copy(bf16[2048,3,512]{2,0,1:T(8,128)(2,1)} %param.27) | data formatting | bytes 12582912 | tf_op args[8]
  17.5 3.2 fusion.44
  20.8 0.2 copy-done.4
  21.0 9.1 %fusion.53 = f32[2,512,3,512]{1,3,2,0:T(8,128)S(1)} fusion(bf16[2048,3,512]{0,2,1:T(8,128)(2,1)} %copy.26, bf16[2,512,2048]{2,1,0:T(8,128)(2,1)S(1)} %copy-done.4, f32[2048]{0:T(1024)S(1)} %copy-done.13, f32[2,512]{1,0:T(2,128)S(1)} %add_rsqrt_fusion.1), kind=kOutput, calls=%fused_computation.55 | convolution fusion | flops 6450839552 | bytes 16789504 | tf_op jit(solution)/shard_map/dot_general | solution.py:64
  30.1 1.7 slice.51
  31.8 1.6 copy-done.9
  33.3 0.1 slice.74
  33.5 0.1 compare_select_fusion.1
  33.6 0.6 gather_fusion.2
  34.2 0.6 gather_fusion.3
  34.9 0.1 broadcast_add_fusion
  35.0 0.6 gather_fusion.4
  35.6 0.3 fusion.73
  36.0 19.5 %all-gather.8.cloned.1.call-done = bf16[64,16,512]{2,1,0:T(8,128)(2,1)} async-done(((bf16[2,16,512]{2,1,0:T(8,128)(2,1)}), bf16[64,16,512]{2,1,0:T(8,128)(2,1)}) %all-gather.8.cloned.1.call-update) | async-done | bytes 1048592 | tf_op jit(solution)/shard_map/all_gather | solution.py:71
  55.4 1.8 gather_fusion.1
  57.2 45.8 %all-gather.6.cloned.1.call-done = bf16[64,16,2048]{2,1,0:T(8,128)(2,1)} async-done(((bf16[2,16,2048]{2,1,0:T(8,128)(2,1)}), bf16[64,16,2048]{2,1,0:T(8,128)(2,1)}) %all-gather.6.cloned.1.call-update) | async-done | bytes 4194320 | tf_op jit(solution)/shard_map/all_gather | solution.py:70
  103.0 2.7 gather_fusion
  105.8 5.8 fusion.61
  111.6 2.9 subtract_convert_fusion
  114.4 1.5 pad_maximum_fusion
  116.0 28.0 %while.11 = (s32[]{:T(128)}, bf16[2,512,8,64]{1,3,2,0:T(8,128)(2,1)}, bf16[2,512,8,64]{1,3,2,0:T(8,128)(2,1)S(1)}, s32[2]{0:T(128)S(1)}, bf16[2,512,8,64]{1,3,2,...) while((s32[]{:T(128)}, bf16[2,512,8,64]{1,3,2,0:T(8,128)(2,1)}, ...), condition=%wide.region_4.6_spmd.clone, body=%wide.region_1.5_spmd.clone.sunk | while | flops 550241280 | bytes 19434588 | solution.py:106
  116.0 0.6 dynamic_slice.68
  116.6 0.6 iota_compare_fusion.5
  117.2 0.1 fusion.115
  117.3 7.6 %fusion.116 = (f32[8,512]{1,0:T(8,128)S(1)}, f32[8,512,512]{1,2,0:T(8,128)}) fusion(pred[512,512]{0,1:T(8,128)(4,1)S(1)} %fusion.115, bf16[2,512,8,64]{1,3,2,0:T(8,128)(2,1)} %get-tuple-element.155, s32[]{:T(128)} %get-tuple-element.143, bf16[2,512,8,64]{1,3,2,0:T(8,128)(2,1)} %get-tuple-element.154), kind=kOutput, calls=%fused_computation.116.clone.1 | convolution fusion | flops 276824576 | bytes 9716736 | tf_op jit(solution)/shard_map/while/body/eval_jaxpr/sub | solution.py:101
  124.9 5.0 fusion.117
  130.0 0.6 dynamic_slice.68
  130.5 0.6 iota_compare_fusion.5
  131.2 0.1 fusion.115
  131.3 7.6 %fusion.116 = (f32[8,512]{1,0:T(8,128)S(1)}, f32[8,512,512]{1,2,0:T(8,128)}) fusion(pred[512,512]{0,1:T(8,128)(4,1)S(1)} %fusion.115, bf16[2,512,8,64]{1,3,2,0:T(8,128)(2,1)} %get-tuple-element.155, s32[]{:T(128)} %get-tuple-element.143, bf16[2,512,8,64]{1,3,2,0:T(8,128)(2,1)} %get-tuple-element.154), kind=kOutput, calls=%fused_computation.116.clone.1 | convolution fusion | flops 276824576 | bytes 9716736 | tf_op jit(solution)/shard_map/while/body/eval_jaxpr/sub | solution.py:101
  138.9 5.0 fusion.117
  143.9 2.3 copy.27
  146.3 0.2 copy.32
  146.5 4.4 convolution_convert_fusion
  151.0 0.5 all-gather.10.cloned.1.call-update
  151.6 0.5 all-gather.12.cloned.1.call-update
  152.2 91.4 %all-reduce.4.cloned.1.call-done = bf16[2,512,2048]{2,1,0:T(8,128)(2,1)} async-done(((bf16[2,512,2048]{2,1,0:T(8,128)(2,1)}), bf16[2,512,2048]{2,1,0:T(8,128)(2,1)}) %all-reduce.4.cloned.1.call-update) | async-done | bytes 4194320 | tf_op jit(solution)/shard_map/psum | solution.py:110
  243.6 5.0 fusion.48
  248.7 0.9 copy-done.6
  249.5 3.6 fusion.50
  253.1 45.4 %all-gather.10.cloned.1.call-done = bf16[2048,2,1024]{2,1,0:T(2,128)(2,1)} async-done(((bf16[64,2,1024]{2,1,0:T(2,128)(2,1)}), bf16[2048,2,1024]{2,1,0:T(2,128)(2,1)}) %all-gather.10.cloned.1.call-update) | async-done | bytes 8388624 | tf_op jit(solution)/shard_map/all_gather | solution.py:119
  298.5 10.3 %copy.33 = bf16[256,8,2,1024]{3,1,2,0:T(8,128)(2,1)} copy(bf16[256,8,2,1024]{3,2,1,0:T(2,128)(2,1)} %bitcast.100) | data formatting | bytes 16777216
  308.8 13.3 %fusion.97 = f32[1024,2048]{1,0:T(8,128)} fusion(bf16[1024,2048]{1,0:T(8,128)(2,1)S(1)} %bitcast.102, bf16[2048,2048]{1,0:T(8,128)(2,1)} %bitcast.101), kind=kOutput, calls=%fused_computation.117 | convolution fusion | flops 8589934592 | bytes 20971520 | tf_op jit(solution)/shard_map/dot_general | solution.py:120
  322.0 24.4 %all-gather.12.cloned.1.call-done = bf16[1024,2048]{0,1:T(8,128)(2,1)} async-done(((bf16[1024,64]{0,1:T(8,128)(2,1)}), bf16[1024,2048]{0,1:T(8,128)(2,1)}) %all-gather.12.cloned.1.call-update) | async-done | bytes 4194320 | tf_op jit(solution)/shard_map/all_gather | solution.py:128
  346.4 11.2 %convolution_convert_fusion.1 = bf16[1024,2048]{1,0:T(8,128)(2,1)} fusion(bf16[1024,2048]{0,1:T(8,128)(2,1)} %all-gather.12.cloned.1.call-done, f32[1024,2048]{1,0:T(8,128)} %fusion.97), kind=kOutput, calls=%fused_computation.61 | convolution fusion | flops 4303355904 | bytes 16777216 | tf_op jit(solution)/shard_map/dot_general | solution.py:126
  357.7 0.6 copy-done.14
  358.3 0.6 dynamic-slice
  359.5 0.1 iota_compare_fusion.3
  359.6 0.1 compare_bitcast_fusion
  359.7 90.6 %all-reduce.6.cloned.1.call-done = bf16[2,512,2048]{2,1,0:T(8,128)(2,1)} async-done(((bf16[2,512,2048]{2,1,0:T(8,128)(2,1)}), bf16[2,512,2048]{2,1,0:T(8,128)(2,1)}) %all-reduce.6.cloned.1.call-update) | async-done | bytes 4194320 | tf_op jit(solution)/shard_map/psum | solution.py:131
  450.3 6.9 %multiply_reduce_fusion = (f32[2]{0:T(128)S(1)}, bf16[2,512,2048]{2,1,0:T(8,128)(2,1)S(1)}) fusion(bf16[2,512,2048]{2,1,0:T(8,128)(2,1)} %all-reduce.6.cloned.1.call-done, bf16[2,512,2048]{2,1,0:T(8,128)(2,1)} %all-reduce.4.cloned.1.call-done, bf16[2,512,2048]{2,1,0:T(8,128)(2,1)} %param.19, pred[2,512]{1,0:T(4,128)(4,1)S(1)} %iota_compare_fusion.3), kind=kLoop, calls=%fused_computation.54 | loop fusion | flops 25165822 | bytes 16778248 | tf_op jit(solution)/shard_map/reduce_sum | solution.py:136
  457.3 2.0 copy-done.7
  459.3 0.7 fusion.82
  459.9 0.1 fusion.78
  460.1 0.1 fusion.80
  460.2 24.8 %all-gather = bf16[32,2,2048]{2,1,0:T(2,128)(2,1)S(1)} all-gather(bf16[1,2,2048]{2,1,0:T(2,128)(2,1)S(1)} %bitcast.109), channel_id=1, replica_groups=mesh['req'=32,'mlp'=4] {'req'}, dimensions={0}, use_global_device_ids=true | all-gather | bytes 270336 | tf_op jit(solution)/shard_map/all_gather | solution.py:143
  484.9 0.1 reshape.230
  485.0 2.1 convolution_reduce_fusion
  487.2 64.5 %pmax.7 = f32[64]{0:T(128)S(1)} all-reduce(f32[64]{0:T(128)S(1)} %convolution_reduce_fusion), channel_id=1, replica_groups=mesh['req'=32,'mlp'=4] {'req','mlp'}, use_global_device_ids=true, to_apply=%region_12.14 | all-reduce | flops 64 | bytes 512 | tf_op jit(solution)/shard_map/pmax | solution.py:152
  551.6 0.1 sqrt_dynamic-update-slice_fusion
  551.7 64.6 %all-reduce = f32[64]{0:T(128)S(1)} all-reduce(f32[64]{0:T(128)S(1)} %sqrt_dynamic-update-slice_fusion), channel_id=1, replica_groups=mesh['req'=32,'mlp'=4] {'req'}, use_global_device_ids=true, to_apply=%add | all-reduce | flops 64 | bytes 512
  616.3 0.6 select_reduce_fusion
  (43 shorter events, 0.4 us)
Async XLA Ops:
  7.2 139.3 %copy-start = (bf16[512,2048]{1,0:T(8,128)(2,1)S(1)}, bf16[512,2048]{1,0:T(8,128)(2,1)}, u32[]{:S(2)}) copy-start(bf16[512,2048]{1,0:T(8,128)(2,1)} %param.28) | copy-start | bytes 6291460
  7.2 48.2 %all-gather.8.cloned.1.call-start = ((), (), s32[]{:S(2)}) async-start(), calls=%async_computation.1 | async-start | bytes 1081344 | tf_op jit(solution)/shard_map/all_gather | solution.py:71
  7.9 95.1 %all-gather.6.cloned.1.call-start = ((), (), s32[]{:S(2)}) async-start(), calls=%async_computation | async-start | bytes 4325376 | tf_op jit(solution)/shard_map/all_gather | solution.py:70
  8.7 234.9 %all-reduce.4.cloned.1.call-start = ((), (), s32[]{:S(2)}) async-start(), calls=%async_computation.2 | async-start | bytes 8388608 | tf_op jit(solution)/shard_map/psum | solution.py:110
  17.5 3.4 copy-start.4
  17.5 3.4 copy-start.13
  30.1 3.3 copy-start.9
  30.1 3.4 copy-start.12
  30.1 3.5 copy-start.1
  30.1 4.1 copy-start.2
  30.1 4.9 copy-start.3
  150.9 147.5 %all-gather.10.cloned.1.call-start = ((), (), s32[]{:S(2)}) async-start(), calls=%async_computation.3 | async-start | bytes 8650752 | tf_op jit(solution)/shard_map/all_gather | solution.py:119
  151.5 194.9 %all-gather.12.cloned.1.call-start = ((), (), s32[]{:S(2)}) async-start(), calls=%async_computation.4 | async-start | bytes 4325376 | tf_op jit(solution)/shard_map/all_gather | solution.py:128
  152.1 96.5 %copy-start.10 = (f32[2048]{0:T(1024)S(1)}, f32[2048]{0:T(1024)}, u32[]{:S(2)}) copy-start(f32[2048]{0:T(1024)} %param.25) | copy-start | bytes 24580
  152.1 298.2 %all-reduce.6.cloned.1.call-start = ((), (), s32[]{:S(2)}) async-start(), calls=%async_computation.5 | async-start | bytes 8388608 | tf_op jit(solution)/shard_map/psum | solution.py:131
  243.6 5.1 copy-start.5
  243.6 5.9 copy-start.6
  298.5 10.3 %copy-start.8 = (bf16[2,512,2048]{2,1,0:T(8,128)(2,1)S(1)}, bf16[2,512,2048]{2,1,0:T(8,128)(2,1)}, u32[]{:S(2)}) copy-start(bf16[2,512,2048]{2,1,0:T(8,128)(2,1)} %fusion.50) | copy-start | bytes 12582916
  357.6 0.7 copy-start.14
  457.3 2.0 copy-start.7
  457.3 2.8 copy-start.11
Sparse Core Ops, SparseCore 0:
  10.3 45.0 all-gather.7
  57.7 45.2 all-gather.5
  151.1 92.4 all-reduce.3
  246.0 52.4 all-gather.9
  300.8 45.5 all-gather.11
  357.8 92.4 all-reduce.5
where the time goes:
time: 624 us
  waiting for transfers between devices  320 us (51%)
  blocking collectives  154 us (25%)
  matrix products  71.7 us (11%)
  local copies, waits for them, and re-layouts  37.1 us (6%)
  other arithmetic  26.4 us (4%)
  between operations  15 us (2%)
    psum x1, waiting for transfers between devices, per_device(): lax.psum(head_part.astype(jnp.bfloat16), 'mlp').astype(jnp.float32)  91.4 us
    psum x1, waiting for transfers between devices, per_device(): lax.psum(unit_part.astype(jnp.bfloat16), 'mlp').astype(jnp.float32)  90.6 us
    unnamed x1, blocking collectives  64.6 us
    pmax x1, blocking collectives, per_device(): slot_peak = lax.pmax(jnp.max(logits, axis=1), ('req', 'mlp'))  64.5 us
    all_gather x1, waiting for transfers between devices, per_device(): lax.all_gather(adapter_down, 'req', axis=0, tiled=True)  45.8 us
    all_gather x1, waiting for transfers between devices, per_device(): shard_piece = lax.all_gather(w_gateup, 'req', axis=0, tiled=True)  45.4 us
    unnamed x35, local copies, waits for them, and re-layouts  25.3 us
    all_gather x1, blocking collectives, per_device(): lax.all_gather(last_normed, 'req', axis=0, tiled=True)  24.8 us
  transfers between devices with their start and end apart: 6, of which 6 were waited for; matrix products, arithmetic and copies ran while one was open for 10% of the time, Pallas kernels for 0%

commit v1 on v0

v1 whole, which is shorter than its diff:
```python
import functools

import jax
import jax.numpy as jnp
import numpy as np
from jax import lax
from jax.experimental import pallas as pl
from jax.experimental.pallas import tpu as pltpu
from jax.sharding import PartitionSpec as P

HEAD_WIDTH = 64
EPSILON = 1e-05
ROPE_BASE = 130000.0
ADAPTER_SCALE = 2.0
MASKED = -1e30
MESH = pl.DeviceIdType.MESH
F32 = jnp.float32
BF16 = jnp.bfloat16
SIDE = 4


def rms_norm(values, gain):
    return values * lax.rsqrt(jnp.mean(values * values, axis=-1, keepdims=True) + EPSILON) * gain


def rope_tables(length):
    half = HEAD_WIDTH // 2
    frequency = ROPE_BASE ** (-(np.arange(half, dtype=np.float64) * 2.0 / HEAD_WIDTH))
    angles = np.arange(length, dtype=np.float64)[:, None] * frequency[None, :]
    cosine, sine = np.cos(angles), np.sin(angles)
    cosines = np.concatenate([cosine, cosine] * 2, axis=1).astype(np.float32)
    sines = np.concatenate([-sine, sine] * 2, axis=1).astype(np.float32)
    return cosines, sines


def dot(a, b):
    return jnp.dot(a, b, preferred_element_type=F32)


def dot_t(a, b):
    return lax.dot_general(a, b, (((1,), (1,)), ((), ())), preferred_element_type=F32)


def layer_kernel(
    rows_ref, gain_attn, gain_mlp, cos_ref, sin_ref,
    hid_h, wqkv_h, wout_h, wts_h, adp_h,
    out_h,
    hid, wqkv, nrm, qb, kb, vb, att, wo, wts, adp, dsel, part, act, outb, xbuf, rbuf, ybuf,
    local_sem, send_sem, recv_sem,
):
    me = lax.axis_index("req")
    z = lax.axis_index("mlp")
    x, y, c = me // 8, (me // 2) % SIDE, me % 2
    nx, px = lax.rem(x + 1, SIDE), lax.rem(x + 3, SIDE)
    ny, py = lax.rem(y + 1, SIDE), lax.rem(y + 3, SIDE)
    nz, pz, oz = lax.rem(z + 1, SIDE), lax.rem(z + 3, SIDE), lax.rem(z + 2, SIDE)
    ox, oy = lax.rem(x + 2, SIDE), lax.rem(y + 2, SIDE)

    def at(xx, yy):
        return (xx * 8 + yy * 2 + c, z)

    xp, xm, yp, ym = at(nx, y), at(px, y), at(x, ny), at(x, py)
    zp, zm, zo = (me, nz), (me, pz), (me, oz)
    twin = (x * 8 + y * 2 + (1 - c), z)

    barrier = pltpu.get_barrier_semaphore()
    for other in (xp, xm, yp, ym, zp, zm, zo, twin):
        pl.semaphore_signal(barrier, inc=1, device_id=other, device_id_type=MESH)
    pl.semaphore_wait(barrier, 8)

    sent = []

    def send(src, dst, to):
        i = len(sent)
        copy = pltpu.make_async_remote_copy(
            src_ref=src, dst_ref=dst, send_sem=send_sem.at[i], recv_sem=recv_sem.at[i],
            device_id=to, device_id_type=MESH,
        )
        copy.start()
        sent.append(copy)
        return copy

    locals_ = []

    def fetch(src, dst):
        copy = pltpu.make_async_copy(src, dst, local_sem.at[len(locals_)])
        copy.start()
        locals_.append(copy)
        return copy

    def gather_xy(src, full):
        width = src.shape[-1] // 2
        left, right = pl.ds(0, width), pl.ds(width, width)
        state = {}

        def step0():
            state["own"] = fetch(src, full.at[x, y, c])
            own_l, own_r = full.at[x, y, c, :, :, left], full.at[x, y, c, :, :, right]
            state["a"] = [
                send(src.at[:, :, left], own_l, xp), send(src.at[:, :, left], own_l, xm),
                send(src.at[:, :, right], own_r, yp), send(src.at[:, :, right], own_r, ym),
            ]

        def step1():
            for copy in state["a"]:
                copy.wait_recv()
            state["b"] = [
                send(full.at[px, y, c, 0:1, :, left], full.at[px, y, c, 0:1, :, left], xp),
                send(full.at[nx, y, c, 1:2, :, left], full.at[nx, y, c, 1:2, :, left], xm),
                send(full.at[x, py, c, 0:1, :, right], full.at[x, py, c, 0:1, :, right], yp),
                send(full.at[x, ny, c, 1:2, :, right], full.at[x, ny, c, 1:2, :, right], ym),
            ]

        def step2():
            state["own"].wait()
            for copy in state["b"]:
                copy.wait_recv()
            line_l, line_r = full.at[:, y, c, :, :, left], full.at[x, :, c, :, :, right]
            state["c"] = [
                send(line_l, line_l, yp), send(line_l, line_l, ym),
                send(line_r, line_r, xp), send(line_r, line_r, xm),
            ]
            state["t"] = [send(line_l, line_l, twin), send(line_r, line_r, twin)]

        def step3():
            for copy in state["c"]:
                copy.wait_recv()
            state["d"] = [
                send(full.at[0:2, py, c, :, :, left], full.at[0:2, py, c, :, :, left], yp),
                send(full.at[2:4, ny, c, :, :, left], full.at[2:4, ny, c, :, :, left], ym),
                send(full.at[px, 0:2, c, :, :, right], full.at[px, 0:2, c, :, :, right], xp),
                send(full.at[nx, 2:4, c, :, :, right], full.at[nx, 2:4, c, :, :, right], xm),
            ]
            for yy in (py, ny):
                state["t"].append(send(full.at[:, yy, c, :, :, left], full.at[:, yy, c, :, :, left], twin))
            for xx in (px, nx):
                state["t"].append(send(full.at[xx, :, c, :, :, right], full.at[xx, :, c, :, :, right], twin))

        def step4():
            for copy in state["d"]:
                copy.wait_recv()
            state["t"].append(send(full.at[:, oy, c, :, :, left], full.at[:, oy, c, :, :, left], twin))
            state["t"].append(send(full.at[ox, :, c, :, :, right], full.at[ox, :, c, :, :, right], twin))

        def step5():
            for copy in state["t"]:
                copy.wait_recv()

        return [step0, step1, step2, step3, step4, step5]

    adp_steps = gather_xy(adp_h, adp)
    wts_steps = gather_xy(wts_h, wts)
    wo_state = {}

    def wo_step0():
        mine = pl.ds(pl.multiple_of(c * 256, 256), 256)
        wo_state["own"] = fetch(wout_h, wo.at[z])
        wo_state["a"] = [
            send(wout_h.at[mine], wo.at[z, mine], zp), send(wout_h.at[mine], wo.at[z, mine], zm),
        ]

    def wo_step1():
        mine = pl.ds(pl.multiple_of(c * 256, 256), 256)
        low = pl.ds(pl.multiple_of(c * 256, 256), 128)
        high = pl.ds(pl.multiple_of(c * 256 + 128, 128), 128)
        for copy in wo_state["a"]:
            copy.wait_recv()
        wo_state["b"] = [
            send(wo.at[pz, low], wo.at[pz, low], zp), send(wo.at[nz, high], wo.at[nz, high], zm),
        ]
        wo_state["t"] = [
            send(wo.at[pz, mine], wo.at[pz, mine], twin), send(wo.at[nz, mine], wo.at[nz, mine], twin),
        ]

    def wo_step2():
        mine = pl.ds(pl.multiple_of(c * 256, 256), 256)
        for copy in wo_state["b"]:
            copy.wait_recv()
        wo_state["t"].append(send(wo.at[oz, mine], wo.at[oz, mine], twin))

    def wo_step3():
        wo_state["own"].wait()
        for copy in wo_state["t"]:
            copy.wait_recv()

    hid_copy = fetch(hid_h, hid)
    adp_steps[0]()
    wqkv_copy = fetch(wqkv_h, wqkv)
    wts_steps[0]()
    wo_step0()

    def normalise(slot, gain):
        def body(i, _):
            rows = pl.ds(pl.multiple_of(i * 32, 32), 32)
            values = hid[slot, rows, :].astype(F32)
            nrm[slot, rows, :] = rms_norm(values, gain[...]).astype(BF16)
            return 0

        lax.fori_loop(0, 16, body, 0)

    lane = lax.broadcasted_iota(jnp.int32, (512, 128), 1)
    first_half = lax.rem(lane, 64) < 32

    def rotate(values):
        swapped = jnp.where(first_half, pltpu.roll(values, 96, 1), pltpu.roll(values, 32, 1))
        return values * cos_ref[...] + swapped * sin_ref[...]

    def keys_values(slot):
        def body(i, _):
            cols = pl.ds(pl.multiple_of(i * 256, 256), 256)
            keys = dot(nrm[slot], wqkv[1, :, cols])
            kb[slot, :, pl.ds(pl.multiple_of(i * 256, 256), 128)] = rotate(keys[:, :128]).astype(BF16)
            kb[slot, :, pl.ds(pl.multiple_of(i * 256 + 128, 128), 128)] = rotate(keys[:, 128:]).astype(BF16)
            vb[slot, :, cols] = dot(nrm[slot], wqkv[2, :, cols]).astype(BF16)
            return 0

        lax.fori_loop(0, 2, body, 0)

    def queries(slot):
        low = dot_t(nrm[slot, :, 0:512], dsel[0, slot])
        for zz in range(1, SIDE):
            low += dot_t(nrm[slot, :, zz * 512:(zz + 1) * 512], dsel[zz, slot])
        low = low.astype(BF16)
        t = rows_ref[slot]
        r = t // 2

        def body(i, _):
            cols = pl.ds(pl.multiple_of(i * 256, 256), 256)
            up = adp[r // 8, (r // 2) % SIDE, r % 2, t % 2][16:32]
            up_low, up_high = up[:, :256], up[:, 256:]
            up_cols = jnp.where(i == 0, up_low, up_high)
            values = dot(nrm[slot], wqkv[0, :, cols]) + ADAPTER_SCALE * dot(low, up_cols)
            scale = HEAD_WIDTH ** (-0.5)
            qb[slot, :, pl.ds(pl.multiple_of(i * 256, 256), 128)] = (rotate(values[:, :128]) * scale).astype(BF16)
            qb[slot, :, pl.ds(pl.multiple_of(i * 256 + 128, 128), 128)] = (rotate(values[:, 128:]) * scale).astype(BF16)
            return 0

        lax.fori_loop(0, 2, body, 0)

    lane_q = lax.broadcasted_iota(jnp.int32, (128, 128), 1) < 64
    causal = lax.broadcasted_iota(jnp.int32, (128, 128), 1) <= lax.broadcasted_iota(jnp.int32, (128, 128), 0)
    causal2 = jnp.concatenate([causal, causal], axis=0)

    def attention(slot):
        def body(i, _):
            cols = pl.ds(pl.multiple_of(i * 128, 128), 128)
            for j in range(4):
                q = qb[slot, j * 128:(j + 1) * 128, cols]
                zero = jnp.zeros_like(q)
                both = jnp.concatenate([jnp.where(lane_q, q, zero), jnp.where(lane_q, zero, q)], axis=0)
                n = (j + 1) * 128
                scores = dot_t(both, kb[slot, 0:n, cols])
                diag = jnp.where(causal2, scores[:, n - 128:], MASKED)
                scores = diag if j == 0 else jnp.concatenate([scores[:, :n - 128], diag], axis=1)
                top = jnp.max(scores, axis=1, keepdims=True)
                weights = jnp.exp(scores - top)
                total = jnp.sum(weights, axis=1, keepdims=True)
                mixed = dot(weights.astype(BF16), vb[slot, 0:n, cols]) / total
                att[slot, z, j * 128:(j + 1) * 128, cols] = jnp.where(lane_q, mixed[:128], mixed[128:]).astype(BF16)
            return 0

        lax.fori_loop(0, 4, body, 0)

    att_state = {}

    def att_send(slot):
        mine = att.at[slot, z]
        att_state[slot] = [send(mine, mine, zp), send(mine, mine, zm)]

    def att_forward(slot):
        for copy in att_state[slot]:
            copy.wait_recv()
        low, high = att.at[slot, pz, 0:256], att.at[slot, nz, 256:512]
        att_state[slot] = [send(low, low, zp), send(high, high, zm)]

    def att_done(slot):
        for copy in att_state[slot]:
            copy.wait_recv()

    hid_copy.wait()
    normalise(0, gain_attn)
    adp_steps[1]()
    normalise(1, gain_attn)
    adp_steps[2]()
    wqkv_copy.wait()
    wts_steps[1]()
    keys_values(0)
    adp_steps[3]()
    keys_values(1)
    adp_steps[4]()
    wts_steps[2]()
    adp_steps[5]()
    for slot in range(2):
        t = rows_ref[slot]
        r = t // 2
        dsel[z, slot] = adp[r // 8, (r // 2) % SIDE, r % 2, t % 2][0:16]
    dsel_copies = [send(dsel.at[z], dsel.at[z], to) for to in (zp, zm, zo)]
    wo_step1()
    for copy in dsel_copies:
        copy.wait_recv()
    queries(0)
    attention(0)
    att_send(0)
    wo_step2()
    wts_steps[3]()
    queries(1)
    attention(1)
    att_send(1)
    wts_steps[4]()
    wo_step3()
    att_forward(0)
    wts_steps[5]()
    att_done(0)

    def project_out(slot):
        def body(i, _):
            cols = pl.ds(pl.multiple_of(i * 256, 256), 256)
            mixed = dot(att[slot, 0], wo[0, :, cols])
            for zz in range(1, SIDE):
                mixed += dot(att[slot, zz], wo[zz, :, cols])
            hid[slot, :, cols] = (hid[slot, :, cols].astype(F32) + mixed).astype(BF16)
            return 0

        lax.fori_loop(0, 8, body, 0)

    def gate_up(slot):
        def body(i, _):
            cols = pl.ds(pl.multiple_of(i * 256, 256), 256)
            up_cols = pl.ds(pl.multiple_of(i * 256 + 1024, 256), 256)
            gate = dot(nrm[slot], wts[:, :, :, :, :, cols].reshape(2048, 256))
            up = dot(nrm[slot], wts[:, :, :, :, :, up_cols].reshape(2048, 256))
            act[:, cols] = (gate / (1.0 + jnp.exp(-gate)) * up).astype(BF16)
            return 0

        lax.fori_loop(0, 4, body, 0)

    def down(slot, half):
        def body(i, _):
            xx = half * 2 + i // 2
            yy = (i % 2) * 2
            weight = wts[pl.ds(xx, 1), pl.ds(yy, 2), :, :, :, 2048:3072].reshape(256, 1024)
            cols = pl.ds(pl.multiple_of(half * 1024 + i * 256, 256), 256)
            part[slot, :, cols] = dot_t(act[...], weight).astype(BF16)
            return 0

        lax.fori_loop(0, 4, body, 0)

    halves = (pl.ds(0, 1024), pl.ds(1024, 1024))

    def block(index):
        return pl.ds(pl.multiple_of(index * 128, 128), 128)

    rs = {}

    def rs_start(slot, half):
        far, near = (zm, zp) if half == 0 else (zp, zm)
        near_z = nz if half == 0 else pz
        rs[slot, half] = [
            send(part.at[slot, block(oz), halves[half]], xbuf.at[slot, half], far),
            send(part.at[slot, block(near_z), halves[half]], rbuf.at[slot, half], near),
        ]

    def rs_middle(slot, half):
        far = zm if half == 0 else zp
        far_z = pz if half == 0 else nz
        rs[slot, half][0].wait_recv()
        xbuf[slot, half] = (
            xbuf[slot, half].astype(F32) + part[slot, block(far_z), halves[half]].astype(F32)
        ).astype(BF16)
        rs[slot, half].append(send(xbuf.at[slot, half], ybuf.at[slot, half], far))

    def rs_finish(slot, half):
        rs[slot, half][1].wait_recv()
        rs[slot, half][2].wait_recv()
        total = part[slot, block(z), halves[half]].astype(F32) + rbuf[slot, half].astype(F32)
        total += ybuf[slot, half].astype(F32) + hid[slot, block(z), halves[half]].astype(F32)
        outb[slot, block(z), halves[half]] = total.astype(BF16)

    ag = {}

    def ag_start(slot):
        mine = outb.at[slot, block(z)]
        ag[slot] = [send(mine, mine, zp), send(mine, mine, zm)]

    def ag_forward(slot):
        for copy in ag[slot]:
            copy.wait_recv()
        left, right = outb.at[slot, block(nz), halves[0]], outb.at[slot, block(pz), halves[1]]
        ag[slot] = [send(left, left, zm), send(right, right, zp)]

    def ag_done(slot):
        for copy in ag[slot]:
            copy.wait_recv()
        fetch(outb.at[slot], out_h.at[slot])

    project_out(0)
    att_forward(1)
    normalise(0, gain_mlp)
    gate_up(0)
    for half in range(2):
        down(0, half)
        rs_start(0, half)
    att_done(1)
    project_out(1)
    normalise(1, gain_mlp)
    for half in range(2):
        rs_middle(0, half)
    gate_up(1)
    for half in range(2):
        rs_finish(0, half)
    ag_start(0)
    for half in range(2):
        down(1, half)
        rs_start(1, half)
    ag_forward(0)
    for half in range(2):
        rs_middle(1, half)
    ag_done(0)
    for half in range(2):
        rs_finish(1, half)
    ag_start(1)
    ag_forward(1)
    ag_done(1)
    for copy in sent:
        copy.wait_send()
    for copy in locals_[-2:]:
        copy.wait()


def layer(table_rows, gain_attn, gain_mlp, hidden, wqkv, wout, weights, adapters):
    cosines, sines = rope_tables(512)
    any_space = pl.BlockSpec(memory_space=pl.ANY)
    vmem = pl.BlockSpec(memory_space=pltpu.VMEM)
    copies = 96
    return pl.pallas_call(
        layer_kernel,
        out_shape=jax.ShapeDtypeStruct((2, 512, 2048), BF16),
        in_specs=[pl.BlockSpec(memory_space=pltpu.SMEM)] + [vmem] * 4 + [any_space] * 5,
        out_specs=any_space,
        scratch_shapes=[
            pltpu.VMEM((2, 512, 2048), BF16),
            pltpu.VMEM((3, 2048, 512), BF16),
            pltpu.VMEM((2, 512, 2048), BF16),
            pltpu.VMEM((2, 512, 512), BF16),
            pltpu.VMEM((2, 512, 512), BF16),
            pltpu.VMEM((2, 512, 512), BF16),
            pltpu.VMEM((2, SIDE, 512, 512), BF16),
            pltpu.VMEM((SIDE, 512, 2048), BF16),
            pltpu.VMEM((SIDE, SIDE, 2, 2, 32, 3072), BF16),
            pltpu.VMEM((SIDE, SIDE, 2, 2, 32, 512), BF16),
            pltpu.VMEM((SIDE, 2, 16, 512), BF16),
            pltpu.VMEM((2, 512, 2048), BF16),
            pltpu.VMEM((512, 1024), BF16),
            pltpu.VMEM((2, 512, 2048), BF16),
            pltpu.VMEM((2, 2, 128, 1024), BF16),
            pltpu.VMEM((2, 2, 128, 1024), BF16),
            pltpu.VMEM((2, 2, 128, 1024), BF16),
            pltpu.SemaphoreType.DMA((8,)),
            pltpu.SemaphoreType.DMA((copies,)),
            pltpu.SemaphoreType.DMA((copies,)),
        ],
        compiler_params=pltpu.CompilerParams(
            collective_id=0, has_side_effects=True, vmem_limit_bytes=67_000_000
        ),
        name="layer",
    )(table_rows, gain_attn[None, :], gain_mlp[None, :], jnp.asarray(cosines), jnp.asarray(sines),
      hidden, wqkv, wout, weights, adapters)


def per_device(
    hidden_in, lengths, slot_request, adapter_of, adapter_slot, norm_gain_attn, norm_gain_mlp, final_gain,
    w_qkv, w_out, w_gateup, w_down, adapter_down, adapter_up, vocab,
):
    req_index = lax.axis_index("req")
    mlp_index = lax.axis_index("mlp")
    slots_number, sequence_length, width = hidden_in.shape
    requests = lax.dynamic_slice_in_dim(slot_request, req_index * slots_number, slots_number)
    own_lengths = jnp.take(lengths, requests)
    table_rows = jnp.take(adapter_slot, jnp.take(adapter_of, requests))
    positions = jnp.arange(sequence_length, dtype=jnp.int32)
    weights = jnp.concatenate([w_gateup.reshape(64, 2048), w_down.T], axis=1).reshape(2, 32, 3072)
    down_quarter = lax.dynamic_slice_in_dim(adapter_down, mlp_index * 512, 512, axis=2)
    adapters = jnp.concatenate([down_quarter, adapter_up], axis=1)
    result = layer(
        table_rows, norm_gain_attn, norm_gain_mlp, hidden_in,
        w_qkv.transpose(1, 0, 2), w_out, weights, adapters,
    )
    live = positions[None, :] < own_lengths[:, None]
    out_hidden = jnp.where(live[:, :, None], result, jnp.zeros_like(result))
    out_float = out_hidden.astype(F32)
    square_sum = jnp.sum(out_float * out_float, axis=(1, 2))
    slot_norm = jnp.sqrt(square_sum / (own_lengths.astype(F32) * width))
    last_rows = jnp.stack([
        lax.dynamic_index_in_dim(result[slot], own_lengths[slot] - 1, 0, keepdims=False)
        for slot in range(slots_number)
    ]).astype(F32)
    last_normed = rms_norm(last_rows, final_gain).astype(BF16)
    every_last = lax.all_gather(last_normed, "req", axis=0, tiled=True)
    logits = lax.dot_general(every_last, vocab, (((1,), (1,)), ((), ())), preferred_element_type=F32)
    own_peak = jnp.max(logits, axis=1)
    padded_norm = jnp.zeros_like(own_peak)
    padded_norm = lax.dynamic_update_slice_in_dim(padded_norm, slot_norm, req_index * slots_number, 0)
    everything = lax.all_gather(jnp.stack([own_peak, padded_norm]), ("req", "mlp"), axis=0, tiled=False)
    slot_peak = jnp.max(everything[:, 0], axis=0)
    every_norm = jnp.max(everything[:, 1], axis=0)
    request_total = slot_request.shape[0]
    owners = slot_request[None, :] == jnp.arange(request_total, dtype=jnp.int32)[:, None]
    request_norm = jnp.sum(jnp.where(owners, every_norm[None, :], 0.0), axis=1)
    request_peak = jnp.sum(jnp.where(owners, slot_peak[None, :], 0.0), axis=1)
    return (out_hidden, request_norm, request_peak)


def solution(mesh):
    return jax.shard_map(
        per_device,
        mesh=mesh,
        in_specs=(
            P("req", None, None), P(), P(), P(), P(), P(), P(), P(),
            P(None, None, "mlp"), P("mlp", None), P("req", None, "mlp"), P("mlp", "req"),
            P("req", None, None), P("req", None, "mlp"), P(("req", "mlp"), None),
        ),
        out_specs=(P("req", None, None), P(), P()),
        check_vma=False,
    )
```

time: 624 us -> 259 us (0.42)
  waiting for transfers between devices: 320 us -> 0 us
  Pallas kernels: 0 us -> 161 us
  blocking collectives: 154 us -> 73.6 us
  matrix products: 71.7 us -> 0.69 us
  local copies, waits for them, and re-layouts: 37.1 us -> 8.85 us
  other arithmetic: 26.4 us -> 10.3 us
  between operations: 15 us -> 3.37 us
    psum x2 -> x0, waiting for transfers between devices: 182 us -> none  [the longest x1 91.4 us: per_device(): lax.psum(head_part.astype(jnp.bfloat16), 'mlp').astype(jnp.float32)]
    pallas_call x0 -> x1, Pallas kernels: none -> 161 us  [layer(): pl.pallas_call(layer_kernel, out_shape=jax.ShapeDtypeStruct((2, 512, 2048...]
    all_gather x4 -> x0, waiting for transfers between devices: 135 us -> none  [the longest x1 45.8 us: per_device(): lax.all_gather(adapter_down, 'req', axis=0, tiled=True)]
    unnamed x1 -> x0, blocking collectives: 64.6 us -> none
    pmax x1 -> x0, blocking collectives: 64.5 us -> none  [per_device(): slot_peak = lax.pmax(jnp.max(logits, axis=1), ('req', 'mlp'))]
    dot_general x9 -> x1, matrix products: 56.6 us -> 0.69 us  [per_device(): lax.dot_general(every_last, vocab, (((1,), (1,)), ((), ())), preferred_el...]
    all_gather x1 -> x2, blocking collectives: 24.8 us -> 73.6 us  [the longest x1 49 us: per_device(): lax.all_gather(jnp.stack([own_peak, padded_norm]), ('req', 'mlp'), axis=0...]
    unnamed x35 -> x11, local copies, waits for them, and re-layouts: 25.3 us -> 0.13 us
  transfers between devices with their start and end apart: 6 -> 0, of which waited for: 6 -> 0; matrix products, arithmetic and copies ran while one was open for 10% -> 0% of each run, Pallas kernels for 0% -> 0%
where the time goes in v1:
time: 259 us; the launch traced here: 258 us
  Pallas kernels  161 us (62%)
  blocking collectives  73.6 us (28%)
  other arithmetic  10.3 us (4%)
  local copies, waits for them, and re-layouts  8.85 us (3%)
  between operations  3.37 us (1%)
    pallas_call x1, Pallas kernels, layer(): pl.pallas_call(layer_kernel, out_shape=jax.ShapeDtypeStruct((2, 512, 2048...  161 us
    all_gather x1, blocking collectives, per_device(): lax.all_gather(jnp.stack([own_peak, padded_norm]), ('req', 'mlp'), axis=0...  49 us
    all_gather x1, blocking collectives, per_device(): every_last = lax.all_gather(last_normed, 'req', axis=0, tiled=True)  24.6 us

profile of v1, /device:TPU:0, one launch (start us, length us, event | category | flops | bytes accessed | tf_op | source)
XLA Modules:
  0.0 257.6 jit_solution(6517613580470797737)
XLA Ops:
  0.6 0.0 copy-start
  0.6 0.0 copy-start.2
  0.7 0.8 compare_select_fusion.1
  1.4 0.0 copy-done
  1.4 0.6 gather_fusion
  2.1 1.3 gather_fusion.1
  3.4 0.7 broadcast_select_fusion.1
  4.1 0.6 fusion.5
  7.3 1.3 gather_fusion.2
  8.6 0.5 and_select_fusion.rows_ref
  9.1 0.8 constant_dynamic-slice_fusion
  9.9 1.4 pad_maximum_fusion.1.adp_h
  11.3 1.1 concatenate.11
  12.4 0.0 copy-done.2
  12.4 0.8 pad_maximum_fusion.wts_h
  13.2 160.7 %layer.1 = bf16[2,512,2048]{2,1,0:T(8,128)(2,1)} custom-call(s32[2]{0:T(128)} %and_select_fusion.rows_ref, f32[1,2048]{1,0:T(1,128)} %bitcast.25, f32[1,2048]{1,0:T(1,128)} %bitcast.26, f32[512,128]{1,0:T(8,128)} %constant.67.clone.cos_ref, f32[512,128]{1,0:T(8,128)} %constant.68.clone.sin_ref, bf16[2,512,2048]{2,1,0:T(8,128)(2,1)} %hid_h.1, ...), custom_call_target="tpu_custom_call" | custom-call | tf_op jit(solution)/shard_map/layer/pallas_call | solution.py:435
  173.9 0.0 copy-start.3
  173.9 0.0 copy-start.1
  173.9 2.8 %fusion.4 = (bf16[1,512,2048]{2,1,0:T(8,128)(2,1)S(1)}, bf16[1,512,2048]{2,1,0:T(8,128)(2,1)S(1)}) fusion(bf16[2,512,2048]{2,1,0:T(8,128)(2,1)} %layer.1), kind=kLoop, calls=%fused_computation.35 | loop fusion | bytes 8388608 | tf_op jit(solution)/shard_map/slice | solution.py:494
  176.8 0.1 fusion
  177.0 0.0 copy-done.3
  177.0 0.1 fusion.3
  177.1 24.6 %all-gather.1 = bf16[32,2,2048]{2,1,0:T(2,128)(2,1)S(1)} all-gather(bf16[1,2,2048]{2,1,0:T(2,128)(2,1)S(1)} %fusion.3), channel_id=1, replica_groups=mesh['req'=32,'mlp'=4] {'req'}, dimensions={0}, use_global_device_ids=true | all-gather | bytes 270336 | tf_op jit(solution)/shard_map/all_gather | solution.py:498
  201.7 0.1 reshape.90
  201.8 0.0 copy-done.1
  201.8 0.7 convolution_reduce_fusion
  202.5 0.1 iota_compare_fusion.1
  202.5 0.0 copy-start.4
  202.5 5.0 %multiply_reduce_fusion = (f32[2]{0:T(128)S(1)}, bf16[2,512,2048]{2,1,0:T(8,128)(2,1)}) fusion(bf16[2,512,2048]{2,1,0:T(8,128)(2,1)} %layer.1, pred[2,512]{1,0:T(4,128)(4,1)S(1)} %iota_compare_fusion.1), kind=kLoop, calls=%fused_computation.3 | loop fusion | flops 8388606 | bytes 8389640 | tf_op jit(solution)/shard_map/reduce_sum | solution.py:491
  207.6 0.1 dynamic_update_slice.4
  207.7 49.0 %all-gather.2 = f32[128,2,64]{2,1,0:T(2,128)S(1)} all-gather(f32[1,2,64]{2,1,0:T(2,128)S(1)} %maximum_bitcast_fusion), channel_id=2, replica_groups=mesh['req'=32,'mlp'=4] {'req','mlp'}, dimensions={0}, use_global_device_ids=true | all-gather | bytes 66048 | tf_op jit(solution)/shard_map/all_gather | solution.py:503
  256.8 0.2 slice_reduce_fusion
  256.9 0.0 copy-done.4
  256.9 0.6 select_reduce_fusion
  (7 shorter events, 0.1 us)
Async XLA Ops:
  0.6 0.8 copy-start
  0.6 11.8 %copy-start.2 = (bf16[1024,64]{0,1:T(8,128)(2,1)S(1)}, bf16[1024,64]{0,1:T(8,128)(2,1)}, u32[]{:S(2)}) copy-start(bf16[1024,64]{0,1:T(8,128)(2,1)} %param.30) | copy-start | bytes 393220
  173.9 3.1 %copy-start.3 = (f32[2048]{0:T(1024)S(1)}, f32[2048]{0:T(1024)}, u32[]{:S(2)}) copy-start(f32[2048]{0:T(1024)} %param.26) | copy-start | bytes 24580
  173.9 27.8 %copy-start.1 = (bf16[384,2048]{1,0:T(8,128)(2,1)S(1)}, bf16[384,2048]{1,0:T(8,128)(2,1)}, u32[]{:S(2)}) copy-start(bf16[384,2048]{1,0:T(8,128)(2,1)} %param.33) | copy-start | bytes 4718596
  202.5 54.4 %copy-start.4 = (s32[64]{0:T(128)S(1)}, s32[64]{0:T(128)}, u32[]{:S(2)}) copy-start(s32[64]{0:T(128)} %param.21) | copy-start | bytes 772

commit v2 on v1

--- a/solution.py
+++ b/solution.py
@@ -42,10 +42,11 @@
 
 
 def layer_kernel(
-    rows_ref, gain_attn, gain_mlp, cos_ref, sin_ref,
-    hid_h, wqkv_h, wout_h, wts_h, adp_h,
-    out_h,
+    lengths_ref, request_ref, adapter_ref, row_ref, gain_attn, gain_mlp, gain_last, cos_ref, sin_ref,
+    hid_h, wqkv_h, wout_h, wts_h, adp_h, vocab_h,
+    out_h, ends_ref,
     hid, wqkv, nrm, qb, kb, vb, att, wo, wts, adp, dsel, part, act, outb, xbuf, rbuf, ybuf,
+    vocab, zbuf, lasts, every, peak_zc, peak_x, peak_y,
     local_sem, send_sem, recv_sem,
 ):
     me = lax.axis_index("req")
@@ -61,12 +62,22 @@
 
     xp, xm, yp, ym = at(nx, y), at(px, y), at(x, ny), at(x, py)
     zp, zm, zo = (me, nz), (me, pz), (me, oz)
-    twin = (x * 8 + y * 2 + (1 - c), z)
+    xo, yo = at(ox, y), at(x, oy)
+    twin_req = x * 8 + y * 2 + (1 - c)
+    twin = (twin_req, z)
+    others_zc = [zp, zm, zo, twin, (twin_req, nz), (twin_req, pz), (twin_req, oz)]
+    others_x, others_y = [xp, xm, xo], [yp, ym, yo]
 
     barrier = pltpu.get_barrier_semaphore()
-    for other in (xp, xm, yp, ym, zp, zm, zo, twin):
+    for other in others_x + others_y + others_zc:
         pl.semaphore_signal(barrier, inc=1, device_id=other, device_id_type=MESH)
-    pl.semaphore_wait(barrier, 8)
+    pl.semaphore_wait(barrier, 13)
+
+    lengths, table_rows = [], []
+    for slot in range(2):
+        request = request_ref[me * 2 + slot]
+        lengths.append(lengths_ref[request])
+        table_rows.append(row_ref[adapter_ref[request]])
 
     sent = []
 
@@ -188,6 +199,7 @@
     wqkv_copy = fetch(wqkv_h, wqkv)
     wts_steps[0]()
     wo_step0()
+    vocab_copy = fetch(vocab_h, vocab)
 
     def normalise(slot, gain):
         def body(i, _):
@@ -221,7 +233,7 @@
         for zz in range(1, SIDE):
             low += dot_t(nrm[slot, :, zz * 512:(zz + 1) * 512], dsel[zz, slot])
         low = low.astype(BF16)
-        t = rows_ref[slot]
+        t = table_rows[slot]
         r = t // 2
 
         def body(i, _):
@@ -291,7 +303,7 @@
     wts_steps[2]()
     adp_steps[5]()
     for slot in range(2):
-        t = rows_ref[slot]
+        t = table_rows[slot]
         r = t // 2
         dsel[z, slot] = adp[r // 8, (r // 2) % SIDE, r % 2, t % 2][0:16]
     dsel_copies = [send(dsel.at[z], dsel.at[z], to) for to in (zp, zm, zo)]
@@ -374,7 +386,13 @@
         rs[slot, half][2].wait_recv()
         total = part[slot, block(z), halves[half]].astype(F32) + rbuf[slot, half].astype(F32)
         total += ybuf[slot, half].astype(F32) + hid[slot, block(z), halves[half]].astype(F32)
-        outb[slot, block(z), halves[half]] = total.astype(BF16)
+        position = lax.broadcasted_iota(jnp.int32, total.shape, 0) + z * 128
+        live = jnp.where(position < lengths[slot], total, 0.0).astype(BF16)
+        outb[slot, block(z), halves[half]] = live
+        live = live.astype(F32)
+        last = jnp.where(position == lengths[slot] - 1, live, 0.0)
+        zbuf[z, slot:slot + 1, halves[half]] = jnp.sum(last, axis=0, keepdims=True)
+        zbuf[z, slot + 2:slot + 3, halves[half]] = jnp.sum(live * live, axis=0, keepdims=True)
 
     ag = {}
 
@@ -418,25 +436,68 @@
     ag_done(0)
     for half in range(2):
         rs_finish(1, half)
+    last_copies = [send(zbuf.at[z], zbuf.at[z], to) for to in (zp, zm, zo)]
     ag_start(1)
+    for copy in last_copies:
+        copy.wait_recv()
+    rows = (zbuf[0] + zbuf[1]) + (zbuf[2] + zbuf[3])
+    squares = jnp.sum(rows, axis=1, keepdims=True)
+    lasts[x, y, c] = rms_norm(rows[0:2], gain_last[...]).astype(BF16)
+    mine = lasts.at[x, y, c]
+    line_copies = [send(mine, mine, to) for to in others_x]
+    for copy in line_copies:
+        copy.wait_recv()
+    line = lasts.at[:, y, c]
+    plane_copies = [send(line, line, to) for to in others_y]
+    twin_copies = [send(line, line, twin)]
     ag_forward(1)
+    for copy in plane_copies:
+        copy.wait_recv()
+    for yy in (ny, py, oy):
+        line = lasts.at[:, yy, c]
+        twin_copies.append(send(line, line, twin))
+    vocab_copy.wait()
+    for copy in twin_copies:
+        copy.wait_recv()
+    for r in range(32):
+        every[2 * r:2 * r + 2, :] = lasts[r // 8, (r // 2) % SIDE, r % 2].astype(F32)
+    logits = dot_t(vocab[...], every[...].astype(BF16))
+    lane_r = lax.broadcasted_iota(jnp.int32, (1, 64), 1)
+    norms = jnp.zeros((1, 64), F32)
+    for slot in range(2):
+        mean = squares[slot + 2:slot + 3] / (lengths[slot].astype(F32) * 2048.0)
+        norms = jnp.where(lane_r == me * 2 + slot, jnp.sqrt(mean), norms)
+    row_r = lax.broadcasted_iota(jnp.int32, (8, 64), 0)
+    peak_zc[z, c] = jnp.where(row_r == 0, jnp.max(logits, axis=0, keepdims=True), norms)
+    peak_copies = [send(peak_zc.at[z, c], peak_zc.at[z, c], to) for to in others_zc]
     ag_done(1)
+    for copy in peak_copies:
+        copy.wait_recv()
+    peak_x[x] = jnp.max(peak_zc[...].reshape(8, 8, 64), axis=0)
+    peak_copies = [send(peak_x.at[x], peak_x.at[x], to) for to in others_x]
+    for copy in peak_copies:
+        copy.wait_recv()
+    peak_y[y] = jnp.max(peak_x[...], axis=0)
+    peak_copies = [send(peak_y.at[y], peak_y.at[y], to) for to in others_y]
+    for copy in peak_copies:
+        copy.wait_recv()
+    ends_ref[...] = jnp.max(peak_y[...], axis=0)
     for copy in sent:
         copy.wait_send()
     for copy in locals_[-2:]:
         copy.wait()
 
 
-def layer(table_rows, gain_attn, gain_mlp, hidden, wqkv, wout, weights, adapters):
+def layer(tables, gains, hidden, wqkv, wout, weights, adapters, vocab):
     cosines, sines = rope_tables(512)
     any_space = pl.BlockSpec(memory_space=pl.ANY)
     vmem = pl.BlockSpec(memory_space=pltpu.VMEM)
-    copies = 96
+    copies = 136
     return pl.pallas_call(
         layer_kernel,
-        out_shape=jax.ShapeDtypeStruct((2, 512, 2048), BF16),
-        in_specs=[pl.BlockSpec(memory_space=pltpu.SMEM)] + [vmem] * 4 + [any_space] * 5,
-        out_specs=any_space,
+        out_shape=(jax.ShapeDtypeStruct((2, 512, 2048), BF16), jax.ShapeDtypeStruct((8, 64), F32)),
+        in_specs=[pl.BlockSpec(memory_space=pltpu.SMEM)] * 4 + [vmem] * 5 + [any_space] * 6,
+        out_specs=(any_space, vmem),
         scratch_shapes=[
             pltpu.VMEM((2, 512, 2048), BF16),
             pltpu.VMEM((3, 2048, 512), BF16),
@@ -455,6 +516,13 @@
             pltpu.VMEM((2, 2, 128, 1024), BF16),
             pltpu.VMEM((2, 2, 128, 1024), BF16),
             pltpu.VMEM((2, 2, 128, 1024), BF16),
+            pltpu.VMEM((384, 2048), BF16),
+            pltpu.VMEM((SIDE, 4, 2048), F32),
+            pltpu.VMEM((SIDE, SIDE, 2, 2, 2048), BF16),
+            pltpu.VMEM((64, 2048), F32),
+            pltpu.VMEM((SIDE, 2, 8, 64), F32),
+            pltpu.VMEM((SIDE, 8, 64), F32),
+            pltpu.VMEM((SIDE, 8, 64), F32),
             pltpu.SemaphoreType.DMA((8,)),
             pltpu.SemaphoreType.DMA((copies,)),
             pltpu.SemaphoreType.DMA((copies,)),
@@ -463,51 +531,25 @@
             collective_id=0, has_side_effects=True, vmem_limit_bytes=67_000_000
         ),
         name="layer",
-    )(table_rows, gain_attn[None, :], gain_mlp[None, :], jnp.asarray(cosines), jnp.asarray(sines),
-      hidden, wqkv, wout, weights, adapters)
+    )(*tables, *(gain[None, :] for gain in gains), jnp.asarray(cosines), jnp.asarray(sines),
+      hidden, wqkv, wout, weights, adapters, vocab)
 
 
 def per_device(
     hidden_in, lengths, slot_request, adapter_of, adapter_slot, norm_gain_attn, norm_gain_mlp, final_gain,
     w_qkv, w_out, w_gateup, w_down, adapter_down, adapter_up, vocab,
 ):
-    req_index = lax.axis_index("req")
     mlp_index = lax.axis_index("mlp")
-    slots_number, sequence_length, width = hidden_in.shape
-    requests = lax.dynamic_slice_in_dim(slot_request, req_index * slots_number, slots_number)
-    own_lengths = jnp.take(lengths, requests)
-    table_rows = jnp.take(adapter_slot, jnp.take(adapter_of, requests))
-    positions = jnp.arange(sequence_length, dtype=jnp.int32)
     weights = jnp.concatenate([w_gateup.reshape(64, 2048), w_down.T], axis=1).reshape(2, 32, 3072)
     down_quarter = lax.dynamic_slice_in_dim(adapter_down, mlp_index * 512, 512, axis=2)
     adapters = jnp.concatenate([down_quarter, adapter_up], axis=1)
-    result = layer(
-        table_rows, norm_gain_attn, norm_gain_mlp, hidden_in,
-        w_qkv.transpose(1, 0, 2), w_out, weights, adapters,
+    out_hidden, ends = layer(
+        (lengths, slot_request, adapter_of, adapter_slot), (norm_gain_attn, norm_gain_mlp, final_gain),
+        hidden_in, w_qkv.transpose(1, 0, 2), w_out, weights, adapters, vocab,
     )
-    live = positions[None, :] < own_lengths[:, None]
-    out_hidden = jnp.where(live[:, :, None], result, jnp.zeros_like(result))
-    out_float = out_hidden.astype(F32)
-    square_sum = jnp.sum(out_float * out_float, axis=(1, 2))
-    slot_norm = jnp.sqrt(square_sum / (own_lengths.astype(F32) * width))
-    last_rows = jnp.stack([
-        lax.dynamic_index_in_dim(result[slot], own_lengths[slot] - 1, 0, keepdims=False)
-        for slot in range(slots_number)
-    ]).astype(F32)
-    last_normed = rms_norm(last_rows, final_gain).astype(BF16)
-    every_last = lax.all_gather(last_normed, "req", axis=0, tiled=True)
-    logits = lax.dot_general(every_last, vocab, (((1,), (1,)), ((), ())), preferred_element_type=F32)
-    own_peak = jnp.max(logits, axis=1)
-    padded_norm = jnp.zeros_like(own_peak)
-    padded_norm = lax.dynamic_update_slice_in_dim(padded_norm, slot_norm, req_index * slots_number, 0)
-    everything = lax.all_gather(jnp.stack([own_peak, padded_norm]), ("req", "mlp"), axis=0, tiled=False)
-    slot_peak = jnp.max(everything[:, 0], axis=0)
-    every_norm = jnp.max(everything[:, 1], axis=0)
-    request_total = slot_request.shape[0]
-    owners = slot_request[None, :] == jnp.arange(request_total, dtype=jnp.int32)[:, None]
-    request_norm = jnp.sum(jnp.where(owners, every_norm[None, :], 0.0), axis=1)
-    request_peak = jnp.sum(jnp.where(owners, slot_peak[None, :], 0.0), axis=1)
-    return (out_hidden, request_norm, request_peak)
+    owners = slot_request[None, :] == jnp.arange(slot_request.shape[0], dtype=jnp.int32)[:, None]
+    by_request = jnp.sum(jnp.where(owners[None], ends[0:2, None, :], 0.0), axis=2)
+    return (out_hidden, by_request[1], by_request[0])
 
 
 def solution(mesh):

time: 259 us -> 185 us (0.71)
  blocking collectives: 73.6 us -> 0 us
  Pallas kernels: 161 us -> 173 us
  other arithmetic: 10.3 us -> 3.17 us
  between operations: 3.37 us -> 0.65 us
    all_gather x2 -> x0, blocking collectives: 73.6 us -> none  [the longest x1 49 us: per_device(): lax.all_gather(jnp.stack([own_peak, padded_norm]), ('req', 'mlp'), axis=0...]
    pallas_call x1, Pallas kernels: 161 us -> 173 us  [layer(): pl.pallas_call(layer_kernel, out_shape=(jax.ShapeDtypeStruct((2, 512, 204...]
    reduce_sum x3 -> x1, other arithmetic: 5.78 us -> 0.09 us  [per_device(): jnp.sum(jnp.where(owners[None], ends[0:2, None, :], 0.0), axis=2)]
    unnamed x11 -> x3, local copies, waits for them, and re-layouts: 0.13 us -> 4.79 us
    gather x3 -> x0, local copies, waits for them, and re-layouts: 3.23 us -> none  [the longest x2 2.59 us: per_device(): table_rows = jnp.take(adapter_slot, jnp.take(adapter_of, requests))]
    slice x2 -> x1, local copies, waits for them, and re-layouts: 3.43 us -> 0.68 us  [per_device(): ends[0:2, None, :]]
where the time goes in v2:
time: 185 us
  Pallas kernels  173 us (94%)
  local copies, waits for them, and re-layouts  7.9 us (4%)
  other arithmetic  3.17 us (2%)
    pallas_call x1, Pallas kernels, layer(): pl.pallas_call(layer_kernel, out_shape=(jax.ShapeDtypeStruct((2, 512, 204...  173 us
    unnamed x3, local copies, waits for them, and re-layouts  4.79 us

profile of v2, /device:TPU:0, one launch (start us, length us, event | category | flops | bytes accessed | tf_op | source)
XLA Modules:
  0.0 184.9 jit_solution(4265795898880023261)
XLA Ops:
  0.6 0.8 constant_dynamic-slice_fusion
  1.4 1.4 pad_maximum_fusion.1.adp_h
  2.8 1.1 concatenate.11
  3.9 1.7 pad_maximum_fusion.wts_h
  5.6 0.0 copy-start
  5.6 173.1 %layer.1 = (bf16[2,512,2048]{2,1,0:T(8,128)(2,1)}, f32[8,64]{1,0:T(8,128)}) custom-call(s32[64]{0:T(128)} %lengths_ref.1, s32[64]{0:T(128)} %request_ref.1, s32[64]{0:T(128)} %adapter_ref.1, s32[64]{0:T(128)} %row_ref.1, f32[1,2048]{1,0:T(1,128)} %bitcast.13, f32[1,2048]{1,0:T(1,128)} %bitcast.14, f32[1,2048]{1,0:T(1,128)} %bitcast.15, ...), custom_call_target="tpu_custom_call" | custom-call | tf_op jit(solution)/shard_map/layer/pallas_call | solution.py:496
  178.8 0.7 slice.9
  179.4 0.0 copy-done
  179.5 0.1 select_reduce_fusion
  179.6 0.5 slice_bitcast_fusion
  180.1 4.8 %copy.21 = bf16[2,512,2048]{2,1,0:T(8,128)(2,1)} copy(bf16[2,512,2048]{2,1,0:T(8,128)(2,1)} %get-tuple-element.12) | data formatting | bytes 8388608
  (1 shorter events, 0.0 us)
Async XLA Ops:
  5.6 173.8 %copy-start = (s32[64]{0:T(128)S(1)}, s32[64]{0:T(128)}, u32[]{:S(2)}) copy-start(s32[64]{0:T(128)} %request_ref.1) | copy-start | bytes 772
